TPU v7x, 32 devices: a whole 2x2x4 slice. The times are simulated.
32 devices in a mesh: expert: 4 (over y, x), dp: 8 (over z, core).
Axes of the slice: x: 2, y: 2, z: 4, core: 2. Of those that a mesh axis runs over, the one named last changes fastest.
Arguments:
- tokens: bfloat16 [1024, 5120], P('dp', 'expert'), may hold values from -6 to 6
- routes: int32 [1024, 2], P('dp'), may hold values from 0 to 7, all different within a row; in each aligned block of 128 rows (0 to 127, 128 to 255, ...) at most 48 rows name the same one
- combine: bfloat16 [1024, 2], P('dp'), may hold values from 0.099609375 to 1
- cotangent: bfloat16 [1024, 5120], P('dp', 'expert'), may hold values from -1.5 to 1.5
- w_gate: bfloat16 [8, 5120, 768], P('dp', 'expert'), may hold values from -0.078125 to 0.078125
- w_up: bfloat16 [8, 5120, 768], P('dp', 'expert'), may hold values from -0.078125 to 0.078125
- w_down: bfloat16 [8, 768, 5120], P('dp', None, 'expert'), may hold values from -0.21875 to 0.21875
Outputs:
- token_grad: bfloat16 [1024, 5120], P('dp', 'expert')
- combine_grad: float32 [1024, 2], P('dp')
- grad_gate: bfloat16 [8, 5120, 768], P('dp', 'expert')
- grad_up: bfloat16 [8, 5120, 768], P('dp', 'expert')
- grad_down: bfloat16 [8, 768, 5120], P('dp', None, 'expert')
Inputs may be any that keep to these rules, and one draw needn't show every extreme that they name: `routes`: each token names 2 different experts. The tokens of one group name any one expert at most 48 times, a bound that some block reaches.
All inputs are finite; a program needn't handle non-finite values.
Results may differ from a plain program's by a relative error of at most 0.018.
Values may be sent and summed in bfloat16 or wider, within the bound.
No kernel may reach another device: no remote copies, remote signals or barrier semaphores. Data moves between devices by JAX's collectives and lax.ppermute only.
A program may use at most 64 MiB of HBM per device.

v0:
```python
import jax
import jax.numpy as jnp
from jax import lax
from jax.sharding import PartitionSpec as P


def contract_last(matrix_a, matrix_b):
    return lax.dot_general(
        matrix_a, matrix_b, (((1,), (1,)), ((), ())), preferred_element_type=jnp.float32
    )


def contract_first(matrix_a, matrix_b):
    return lax.dot_general(
        matrix_a, matrix_b, (((0,), (0,)), ((), ())), preferred_element_type=jnp.float32
    )


def swiglu_grads(pre_gate, pre_up, back_hidden, weights):
    sigmas = jax.nn.sigmoid(pre_gate)
    active = pre_gate * sigmas
    hidden = (active * pre_up).astype(jnp.bfloat16)
    scaled = weights[:, None] * back_hidden
    grad_gate_pre = (scaled * pre_up * sigmas * (1.0 + pre_gate * (1.0 - sigmas))).astype(
        jnp.bfloat16
    )
    grad_up_pre = (scaled * active).astype(jnp.bfloat16)
    return (hidden, grad_gate_pre, grad_up_pre)


def body(tokens, routes, combine, cotangent, w_gate, w_up, w_down):
    tok_rows, slice_width = tokens.shape
    top_routes = routes.shape[1]
    experts = lax.axis_size("dp")
    capacity = 3 * tok_rows * top_routes // (2 * experts)
    route_count = tok_rows * top_routes
    slot_total = experts * capacity
    route_flat = routes.reshape(route_count)
    onehot = (route_flat[:, None] == jnp.arange(experts, dtype=jnp.int32)[None, :]).astype(
        jnp.int32
    )
    slot_rank = jnp.sum((jnp.cumsum(onehot, axis=0) - onehot) * onehot, axis=1)
    places = route_flat * capacity + slot_rank
    source = jnp.full((slot_total,), route_count, jnp.int32)
    source = source.at[places].set(jnp.arange(route_count, dtype=jnp.int32))
    blank_row = jnp.zeros((1, slice_width), jnp.bfloat16)
    token_send = jnp.concatenate([tokens, blank_row], axis=0)[source // top_routes]
    cot_send = jnp.concatenate([cotangent, blank_row], axis=0)[source // top_routes]
    comb_send = jnp.concatenate(
        [combine.reshape(route_count), jnp.zeros((1,), jnp.bfloat16)], axis=0
    )[source]
    arrived_tok, arrived_cot, arrived_comb = (
        lax.all_to_all(
            token_send.reshape(experts, capacity, slice_width),
            "dp",
            split_axis=0,
            concat_axis=0,
            tiled=True,
        ),
        lax.all_to_all(
            cot_send.reshape(experts, capacity, slice_width),
            "dp",
            split_axis=0,
            concat_axis=0,
            tiled=True,
        ),
        lax.all_to_all(
            comb_send.reshape(experts, capacity), "dp", split_axis=0, concat_axis=0, tiled=True
        ),
    )
    token_slots = arrived_tok.reshape(slot_total, slice_width)
    cot_slots = arrived_cot.reshape(slot_total, slice_width)
    comb_slots = arrived_comb.reshape(slot_total).astype(jnp.float32)
    gate_mat = w_gate[0]
    up_mat = w_up[0]
    down_mat = w_down[0]
    partials = jnp.stack(
        [
            jnp.dot(token_slots, gate_mat, preferred_element_type=jnp.float32),
            jnp.dot(token_slots, up_mat, preferred_element_type=jnp.float32),
            contract_last(cot_slots, down_mat),
        ],
        axis=1,
    )
    summed = lax.psum_scatter(
        partials.astype(jnp.bfloat16), "expert", scatter_dimension=2, tiled=True
    ).astype(jnp.float32)
    hidden_part, gate_part, up_part = swiglu_grads(
        summed[:, 0], summed[:, 1], summed[:, 2], comb_slots
    )
    slot_comb = jnp.sum(hidden_part.astype(jnp.float32) * summed[:, 2], axis=1)
    joined = lax.all_gather(
        jnp.stack([hidden_part, gate_part, up_part], axis=1), "expert", axis=2, tiled=True
    )
    hidden = joined[:, 0]
    grad_gate_pre = joined[:, 1]
    grad_up_pre = joined[:, 2]
    slot_dx = contract_last(grad_gate_pre, gate_mat) + contract_last(grad_up_pre, up_mat)
    scaled_dy = (comb_slots[:, None] * cot_slots.astype(jnp.float32)).astype(jnp.bfloat16)
    grad_gate = contract_first(token_slots, grad_gate_pre).astype(jnp.bfloat16)[None]
    grad_up = contract_first(token_slots, grad_up_pre).astype(jnp.bfloat16)[None]
    grad_down = contract_first(hidden, scaled_dy).astype(jnp.bfloat16)[None]
    back_dx, back_comb = (
        lax.all_to_all(
            slot_dx.reshape(experts, capacity, slice_width).astype(jnp.bfloat16),
            "dp",
            split_axis=0,
            concat_axis=0,
            tiled=True,
        ).astype(jnp.float32),
        lax.all_to_all(
            slot_comb.reshape(experts, capacity).astype(jnp.bfloat16),
            "dp",
            split_axis=0,
            concat_axis=0,
            tiled=True,
        ).astype(jnp.float32),
    )
    route_dx = back_dx.reshape(slot_total, slice_width)[places].reshape(
        tok_rows, top_routes, slice_width
    )
    token_grad = jnp.sum(route_dx, axis=1).astype(jnp.bfloat16)
    comb_part = back_comb.reshape(slot_total)[places].reshape(tok_rows, top_routes)
    combine_grad = lax.psum(comb_part, "expert")
    return (token_grad, combine_grad, grad_gate, grad_up, grad_down)


def solution(mesh):
    in_specs = (
        P("dp", "expert"),
        P("dp", None),
        P("dp", None),
        P("dp", "expert"),
        P("dp", "expert", None),
        P("dp", "expert", None),
        P("dp", None, "expert"),
    )
    out_specs = (
        P("dp", "expert"),
        P("dp", None),
        P("dp", "expert", None),
        P("dp", "expert", None),
        P("dp", None, "expert"),
    )
    return jax.shard_map(body, mesh=mesh, in_specs=in_specs, out_specs=out_specs, check_vma=False)
```

profile of v0, /device:TPU:0, one launch (start us, length us, event | category | flops | bytes accessed | tf_op | source)
XLA Modules:
  0.0 218.3 jit_solution(15409593457587932573)
XLA Ops:
  10.3 1.4 scatter_custom_fusion
  12.7 2.8 %gather_fusion = bf16[384,1280]{1,0:T(8,128)(2,1)} fusion(bf16[129,1280]{1,0:T(8,128)(2,1)S(1)} %concatenate.9, s32[1024]{0:T(1024)S(1)} %get-tuple-element.26), kind=kCustom, calls=%fused_computation | custom fusion | bytes 1967616 | tf_op jit(solution)/shard_map/gather | solution.py:47
  15.5 6.3 %all-to-all-start = ((bf16[8,48,1280]{2,1,0:T(8,128)(2,1)}), bf16[8,48,1280]{2,1,0:T(8,128)(2,1)S(1)}, u32[]{:S(2)}, u32[]{:S(2)}) async-start(bf16[8,48,1280]{2,1,0:T(8,128)(2,1)} %bitcast.4), calls=%async_computation | async-start | bytes 1966080 | tf_op jit(solution)/shard_map/all_to_all | solution.py:53
  22.8 2.8 %gather_fusion.1 = bf16[384,1280]{1,0:T(8,128)(2,1)} fusion(bf16[129,1280]{1,0:T(8,128)(2,1)S(1)} %concatenate.10, s32[1024]{0:T(1024)S(1)} %get-tuple-element.26), kind=kCustom, calls=%fused_computation.1 | custom fusion | bytes 1967616 | tf_op jit(solution)/shard_map/gather | solution.py:48
  25.6 21.4 %all-to-all-done = bf16[8,48,1280]{2,1,0:T(8,128)(2,1)S(1)} async-done(((bf16[8,48,1280]{2,1,0:T(8,128)(2,1)}), bf16[8,48,1280]{2,1,0:T(8,128)(2,1)S(1)}, u32[]{:S(2)}, u32[]{:S(2)}) %all-to-all-start) | async-done | bytes 983072 | tf_op jit(solution)/shard_map/all_to_all | solution.py:53
  48.0 3.6 %all-to-all-start.1 = ((bf16[8,48,1280]{2,1,0:T(8,128)(2,1)}), bf16[8,48,1280]{2,1,0:T(8,128)(2,1)S(1)}, u32[]{:S(2)}, u32[]{:S(2)}) async-start(bf16[8,48,1280]{2,1,0:T(8,128)(2,1)} %bitcast.107), calls=%async_computation.1 | async-start | bytes 1966080 | tf_op jit(solution)/shard_map/all_to_all | solution.py:60
  51.6 2.9 %fusion.25 = bf16[384,1,768]{2,0,1:T(8,128)(2,1)S(1)} fusion(bf16[384,1280]{1,0:T(8,128)(2,1)} %bitcast.109, bf16[1,1280,768]{2,1,0:T(8,128)(2,1)} %param.12), kind=kOutput, calls=%fused_computation.29 | convolution fusion | flops 755269632 | bytes 3538944 | tf_op jit(solution)/shard_map/dot_general | solution.py:80
  54.5 1.7 fusion.28
  56.2 20.4 %all-to-all-done.1 = bf16[8,48,1280]{2,1,0:T(8,128)(2,1)S(1)} async-done(((bf16[8,48,1280]{2,1,0:T(8,128)(2,1)}), bf16[8,48,1280]{2,1,0:T(8,128)(2,1)S(1)}, u32[]{:S(2)}, u32[]{:S(2)}) %all-to-all-start.1) | async-done | bytes 983072 | tf_op jit(solution)/shard_map/all_to_all | solution.py:60
  76.6 2.9 %fusion.22 = bf16[384,1,768]{2,0,1:T(8,128)(2,1)S(1)} fusion(bf16[384,1280]{1,0:T(8,128)(2,1)S(1)} %bitcast.106, bf16[1,768,1280]{2,1,0:T(8,128)(2,1)} %param.13), kind=kOutput, calls=%fused_computation.28 | convolution fusion | flops 755269632 | bytes 3538944 | tf_op jit(solution)/shard_map/dot_general | solution.py:8
  79.5 1.4 pad_maximum_fusion
  81.0 5.2 %copy.32 = bf16[384,3,768]{0,1,2:T(4,128)(2,1)} copy(bf16[384,3,768]{2,0,1:T(8,128)(2,1)} %pad_maximum_fusion) | data formatting | bytes 3538944
  86.2 3.2 %copy.34 = bf16[96,8,3,384]{3,1,2,0:T(8,128)(2,1)} copy(bf16[96,8,3,384]{3,2,1,0:T(4,128)(2,1)} %bitcast.104) | data formatting | bytes 3538944
  89.7 2.8 %gather_fusion.2 = bf16[384]{0:T(512)(128)(2,1)S(1)} fusion(bf16[257]{0:T(512)(128)(2,1)S(1)} %pad_maximum_fusion.2, s32[1024]{0:T(1024)S(1)} %get-tuple-element.25), kind=kCustom, calls=%fused_computation.2 | custom fusion | bytes 3072 | tf_op jit(solution)/shard_map/gather | solution.py:49
  92.6 7.9 %all_to_all.31 = bf16[8,1,48]{2,1,0:T(2,128)(2,1)S(1)} all-to-all(bf16[8,1,48]{2,1,0:T(2,128)(2,1)S(1)} %all_to_all.25), channel_id=1, replica_groups=mesh['expert'=4,'dp'=8] {'dp'}, dimensions={0} | all-to-all | bytes 1536 | tf_op jit(solution)/shard_map/all_to_all | solution.py:67
  100.6 20.2 %reduce-scatter.4.cloned.1.call-done = bf16[192,1152]{1,0:T(8,128)(2,1)} async-done(((bf16[768,1152]{1,0:T(8,128)(2,1)}), bf16[192,1152]{1,0:T(8,128)(2,1)}) %reduce-scatter.4.cloned.1.call-update) | async-done | bytes 442384
  120.9 1.4 reshape.204
  126.0 2.1 copy.29
  129.0 4.6 %all-to-all-start.4 = ((bf16[8,1,48]{2,1,0:T(2,128)(2,1)}), bf16[8,1,48]{2,1,0:T(2,128)(2,1)S(1)}, u32[]{:S(2)}, u32[]{:S(2)}) async-start(bf16[8,1,48]{2,1,0:T(2,128)(2,1)} %convert_element_type.121), calls=%async_computation.4 | async-start | bytes 8192 | tf_op jit(solution)/shard_map/all_to_all | solution.py:111
  133.6 27.2 %all-gather.2.cloned.1.call-done = bf16[384,3,768]{0,2,1:T(8,128)(2,1)} async-done(((bf16[384,3,192]{0,2,1:T(8,128)(2,1)}), bf16[384,3,768]{0,2,1:T(8,128)(2,1)}) %all-gather.2.cloned.1.call-update) | async-done | bytes 1769488 | tf_op jit(solution)/shard_map/all_gather | solution.py:92
  160.8 2.2 %fusion.9 = f32[384,1280]{1,0:T(8,128)S(1)} fusion(bf16[1,1280,768]{2,1,0:T(8,128)(2,1)S(1)} %copy-done, bf16[384,3,768]{0,2,1:T(8,128)(2,1)} %all-gather.2.cloned.1.call-done), kind=kOutput, calls=%fused_computation.19 | convolution fusion | flops 754974720 | bytes 4521984 | tf_op jit(solution)/shard_map/dot_general | solution.py:8
  163.0 3.1 %fusion.3 = bf16[384,1280]{1,0:T(8,128)(2,1)} fusion(f32[384,1280]{1,0:T(8,128)S(1)} %fusion.9, bf16[1,1280,768]{2,1,0:T(8,128)(2,1)S(1)} %copy-done.9, bf16[384,3,768]{0,2,1:T(8,128)(2,1)} %all-gather.2.cloned.1.call-done), kind=kOutput, calls=%fused_computation.13 | convolution fusion | flops 755957760 | bytes 5505024 | tf_op jit(solution)/shard_map/dot_general | solution.py:8
  166.1 4.7 %all-to-all-start.3 = ((bf16[8,48,1280]{2,1,0:T(8,128)(2,1)}), bf16[8,48,1280]{2,1,0:T(8,128)(2,1)}, u32[]{:S(2)}, u32[]{:S(2)}) async-start(bf16[8,48,1280]{2,1,0:T(8,128)(2,1)} %bitcast.113), calls=%async_computation.3 | async-start | bytes 1966080 | tf_op jit(solution)/shard_map/all_to_all | solution.py:104
  172.1 1.9 gather_fusion.4
  174.2 16.2 %psum.7 = f32[128,2]{1,0:T(8,128)S(1)} all-reduce(f32[128,2]{1,0:T(8,128)S(1)} %reshape.146), channel_id=1, replica_groups=mesh['expert'=4,'dp'=8] {'expert'}, use_global_device_ids=true, to_apply=%region_7.8 | all-reduce | flops 256 | bytes 2048 | tf_op jit(solution)/shard_map/psum | solution.py:124
  191.0 4.0 %fusion = bf16[1,1280,768]{2,1,0:T(8,128)(2,1)} fusion(bf16[384,1280]{1,0:T(8,128)(2,1)} %bitcast.110, bf16[384,3,768]{0,2,1:T(8,128)(2,1)} %all-gather.2.cloned.1.call-done), kind=kOutput, calls=%fused_computation.10 | convolution fusion | flops 755957760 | bytes 3538944 | tf_op jit(solution)/shard_map/dot_general | solution.py:14
  195.0 2.5 %fusion.1 = bf16[1,1280,768]{2,1,0:T(8,128)(2,1)} fusion(bf16[384,1280]{1,0:T(8,128)(2,1)S(1)} %bitcast.112, bf16[384,3,768]{0,2,1:T(8,128)(2,1)S(1)} %copy-done.10), kind=kOutput, calls=%fused_computation.11 | convolution fusion | flops 755957760 | bytes 3538944 | tf_op jit(solution)/shard_map/dot_general | solution.py:14
  197.6 2.4 %fusion.2 = bf16[1,768,1280]{2,1,0:T(8,128)(2,1)} fusion(bf16[384,1280]{1,0:T(8,128)(2,1)S(1)} %bitcast.114, bf16[384,3,768]{0,2,1:T(8,128)(2,1)S(1)} %copy-done.10), kind=kOutput, calls=%fused_computation.12 | convolution fusion | flops 755957760 | bytes 3538944 | tf_op jit(solution)/shard_map/dot_general | solution.py:14
  200.0 2.6 %bitcast_convert_fusion = f32[384,1280]{1,0:T(8,128)} fusion(bf16[8,48,1280]{2,1,0:T(8,128)(2,1)} %all-to-all-done.3), kind=kLoop, calls=%fused_computation.31 | loop fusion | flops 491520 | bytes 2949120 | tf_op jit(solution)/shard_map/reshape | solution.py:119
  202.6 3.3 %gather_fusion.3 = f32[256,1280]{1,0:T(8,128)S(1)} fusion(f32[384,1280]{1,0:T(8,128)} %bitcast_convert_fusion, s32[1024]{0:T(1024)S(1)} %pad_clamp_fusion), kind=kCustom, calls=%fused_computation.3 | custom fusion | bytes 2622464 | tf_op jit(solution)/shard_map/gather | solution.py:119
  206.0 1.8 reshape.145
  207.8 3.6 %reduce_sum.31 = bf16[128,1280]{1,0:T(8,128)(2,1)} reduce(f32[128,2,1280]{2,1,0:T(2,128)} %reshape.145, f32[]{:T(128)} %constant.40.clone.1), dimensions={1}, to_apply=%region_5.6 | reduce | flops 163840 | bytes 1638404 | tf_op jit(solution)/shard_map/reduce_sum | solution.py:122
  (65 shorter events, 13.3 us)
Async XLA Ops:
  7.2 47.3 %copy-start = (bf16[1,1280,768]{2,1,0:T(8,128)(2,1)S(1)}, bf16[1,1280,768]{2,1,0:T(8,128)(2,1)}, u32[]{:S(2)}) copy-start(bf16[1,1280,768]{2,1,0:T(8,128)(2,1)} %param.11) | copy-start | bytes 5898244
  15.5 31.5 %all-to-all-start = ((bf16[8,48,1280]{2,1,0:T(8,128)(2,1)}), bf16[8,48,1280]{2,1,0:T(8,128)(2,1)S(1)}, u32[]{:S(2)}, u32[]{:S(2)}) async-start(bf16[8,48,1280]{2,1,0:T(8,128)(2,1)} %bitcast.4), calls=%async_computation | async-start | bytes 1966080 | tf_op jit(solution)/shard_map/all_to_all | solution.py:53
  47.0 0.9 copy-start.3
  48.0 28.7 %all-to-all-start.1 = ((bf16[8,48,1280]{2,1,0:T(8,128)(2,1)}), bf16[8,48,1280]{2,1,0:T(8,128)(2,1)S(1)}, u32[]{:S(2)}, u32[]{:S(2)}) async-start(bf16[8,48,1280]{2,1,0:T(8,128)(2,1)} %bitcast.107), calls=%async_computation.1 | async-start | bytes 1966080 | tf_op jit(solution)/shard_map/all_to_all | solution.py:60
  51.5 69.4 %reduce-scatter.4.cloned.1.call-start = ((), (), s32[]{:S(2)}) async-start(), calls=%async_computation.7 | async-start | bytes 2211840
  51.6 2.9 %copy-start.4 = (bf16[8,48,1280]{2,1,0:T(8,128)(2,1)S(1)}, bf16[8,48,1280]{2,1,0:T(8,128)(2,1)}, u32[]{:S(2)}) copy-start(bf16[8,48,1280]{2,1,0:T(8,128)(2,1)} %copy-done.3) | copy-start | bytes 2949124
  76.6 2.9 %copy-start.1 = (bf16[8,48,1280]{2,1,0:T(8,128)(2,1)}, bf16[8,48,1280]{2,1,0:T(8,128)(2,1)S(1)}, u32[]{:S(2)}) copy-start(bf16[8,48,1280]{2,1,0:T(8,128)(2,1)S(1)} %all-to-all-done.1) | copy-start | bytes 2949124
  76.6 2.9 %copy-start.7 = (bf16[384,1,768]{2,0,1:T(8,128)(2,1)S(1)}, bf16[384,1,768]{2,0,1:T(8,128)(2,1)}, u32[]{:S(2)}) copy-start(bf16[384,1,768]{2,0,1:T(8,128)(2,1)} %fusion.28) | copy-start | bytes 1769476
  86.1 3.3 %copy-start.8 = (bf16[128,2]{0,1:T(2,128)(2,1)S(1)}, bf16[128,2]{0,1:T(2,128)(2,1)}, u32[]{:S(2)}) copy-start(bf16[128,2]{0,1:T(2,128)(2,1)} %param.9) | copy-start | bytes 1540
  89.4 71.4 %all-gather.2.cloned.1.call-start = ((), (), s32[]{:S(2)}) async-start(), calls=%async_computation.6 | async-start | bytes 2211840 | tf_op jit(solution)/shard_map/all_gather | solution.py:92
  129.0 37.1 %all-to-all-start.4 = ((bf16[8,1,48]{2,1,0:T(2,128)(2,1)}), bf16[8,1,48]{2,1,0:T(2,128)(2,1)S(1)}, u32[]{:S(2)}, u32[]{:S(2)}) async-start(bf16[8,1,48]{2,1,0:T(2,128)(2,1)} %convert_element_type.121), calls=%async_computation.4 | async-start | bytes 8192 | tf_op jit(solution)/shard_map/all_to_all | solution.py:111
  160.8 2.2 %copy-start.9 = (bf16[1,1280,768]{2,1,0:T(8,128)(2,1)S(1)}, bf16[1,1280,768]{2,1,0:T(8,128)(2,1)}, u32[]{:S(2)}) copy-start(bf16[1,1280,768]{2,1,0:T(8,128)(2,1)} %param.12) | copy-start | bytes 5898244
  166.1 4.8 %copy-start.2 = (bf16[8,48,1280]{2,1,0:T(8,128)(2,1)S(1)}, bf16[8,48,1280]{2,1,0:T(8,128)(2,1)}, u32[]{:S(2)}) copy-start(bf16[8,48,1280]{2,1,0:T(8,128)(2,1)} %copy-done.1) | copy-start | bytes 2949124
  166.1 33.9 %all-to-all-start.3 = ((bf16[8,48,1280]{2,1,0:T(8,128)(2,1)}), bf16[8,48,1280]{2,1,0:T(8,128)(2,1)}, u32[]{:S(2)}, u32[]{:S(2)}) async-start(bf16[8,48,1280]{2,1,0:T(8,128)(2,1)} %bitcast.113), calls=%async_computation.3 | async-start | bytes 1966080 | tf_op jit(solution)/shard_map/all_to_all | solution.py:104
  174.2 20.8 %copy-start.5 = (bf16[8,48,1280]{2,1,0:T(8,128)(2,1)S(1)}, bf16[8,48,1280]{2,1,0:T(8,128)(2,1)}, u32[]{:S(2)}) copy-start(bf16[8,48,1280]{2,1,0:T(8,128)(2,1)} %copy-done.3) | copy-start | bytes 2949124
  191.0 4.0 %copy-start.10 = (bf16[384,3,768]{0,2,1:T(8,128)(2,1)S(1)}, bf16[384,3,768]{0,2,1:T(8,128)(2,1)}, u32[]{:S(2)}) copy-start(bf16[384,3,768]{0,2,1:T(8,128)(2,1)} %all-gather.2.cloned.1.call-done) | copy-start | bytes 5308420
  195.0 2.5 %copy-start.6 = (bf16[8,48,1280]{2,1,0:T(8,128)(2,1)S(1)}, bf16[8,48,1280]{2,1,0:T(8,128)(2,1)}, u32[]{:S(2)}) copy-start(bf16[8,48,1280]{2,1,0:T(8,128)(2,1)} %multiply_convert_fusion) | copy-start | bytes 2949124
Sparse Core Ops, SparseCore 0:
  89.5 31.3 reduce-scatter.3
  128.2 32.5 all-gather.1
where the time goes:
time: 219 us; the launch traced here: 218 us
  waiting for transfers between devices  89.4 us (41%)
  local copies, waits for them, and re-layouts  36.5 us (17%)
  blocking collectives  24.1 us (11%)
  matrix products  21.7 us (10%)
  starting transfers between devices  19.3 us (9%)
  between operations  14.3 us (7%)
  other arithmetic  13 us (6%)
    all_gather x1, waiting for transfers between devices, body(): lax.all_gather(jnp.stack([hidden_part, gate_part, up_part], axis=1), 'exp...  27.2 us
    all_to_all x1, waiting for transfers between devices, body(): lax.all_to_all(token_send.reshape(experts, capacity, slice_width), 'dp',...  21.4 us
    all_to_all x1, waiting for transfers between devices, body(): lax.all_to_all(cot_send.reshape(experts, capacity, slice_width), 'dp', sp...  20.4 us
    unnamed x3, waiting for transfers between devices  20.3 us
    psum x1, blocking collectives, body(): combine_grad = lax.psum(comb_part, 'expert')  16.2 us
    unnamed x29, local copies, waits for them, and re-layouts  13.6 us
    dot_general x3, matrix products, contract_first(): lax.dot_general(matrix_a, matrix_b, (((0,), (0,)), ((), ())), preferred_e...  8.94 us
    dot_general x3, matrix products, contract_last(): lax.dot_general(matrix_a, matrix_b, (((1,), (1,)), ((), ())), preferred_e...  8.15 us
  transfers between devices with their start and end apart: 6, of which 4 were waited for; matrix products, arithmetic and copies ran while one was open for 14% of the time, Pallas kernels for 0%

commit v1 on v0

--- a/solution.py
+++ b/solution.py
@@ -1,7 +1,28 @@
+import functools
 import jax
 import jax.numpy as jnp
 from jax import lax
 from jax.sharding import PartitionSpec as P
+from jax.lax import axis_index, axis_size, ppermute
+
+
+def run_the_values(page, axis_key):
+    row_out, p_next = (axis_size(axis_key), axis_index(axis_key))
+    outcome_arr = page.shape[0] // row_out
+    w1 = list(page.shape)
+    w1[0] = outcome_arr
+    extra = w1[0]
+    w1[0] = extra * row_out
+    x_next = jnp.zeros(w1, page.dtype)
+    for rr in tuple(range(row_out)):
+        oldest = lax.dynamic_slice_in_dim(page, (p_next ^ rr) * outcome_arr, outcome_arr, axis=0)
+        if rr:
+            oldest = ppermute(oldest, axis_key, [(d, d ^ rr) for d in range(row_out)])
+        x_next = lax.dynamic_update_slice_in_dim(x_next, oldest, (p_next ^ rr) * extra, axis=0)
+    return x_next
+
+
+record_convert = functools.partial(run_the_values, axis_key="dp")
 
 
 def contract_last(matrix_a, matrix_b):
@@ -101,13 +122,9 @@
     grad_up = contract_first(token_slots, grad_up_pre).astype(jnp.bfloat16)[None]
     grad_down = contract_first(hidden, scaled_dy).astype(jnp.bfloat16)[None]
     back_dx, back_comb = (
-        lax.all_to_all(
-            slot_dx.reshape(experts, capacity, slice_width).astype(jnp.bfloat16),
-            "dp",
-            split_axis=0,
-            concat_axis=0,
-            tiled=True,
-        ).astype(jnp.float32),
+        record_convert(slot_dx.reshape(experts, capacity, slice_width).astype(jnp.bfloat16)).astype(
+            jnp.float32
+        ),
         lax.all_to_all(
             slot_comb.reshape(experts, capacity).astype(jnp.bfloat16),
             "dp",

time: 219 us -> 208 us (0.950); the launches traced: 218 us -> 204 us
  waiting for transfers between devices: 89.4 us -> 75.1 us
  matrix products: 21.7 us -> 18.1 us
  starting transfers between devices: 19.3 us -> 22.8 us
    all_gather x1, waiting for transfers between devices: 27.2 us -> 2.67 us  [body(): lax.all_gather(jnp.stack([hidden_part, gate_part, up_part], axis=1), 'exp...]
    ppermute x0 -> x7, starting transfers between devices: none -> 8.19 us  [run_the_values(): oldest = ppermute(oldest, axis_key, [(d, d ^ rr) for d in range(row_out)])]
    ppermute x0 -> x7, waiting for transfers between devices: none -> 6.31 us  [run_the_values(): oldest = ppermute(oldest, axis_key, [(d, d ^ rr) for d in range(row_out)])]
    all_to_all x1 -> x0, starting transfers between devices: 4.75 us -> none  [body(): lax.all_to_all(slot_dx.reshape(experts, capacity, slice_width).astype(jnp...]
    all_to_all x1, waiting for transfers between devices: 0.01 us -> 4 us  [body(): lax.all_to_all(slot_comb.reshape(experts, capacity).astype(jnp.bfloat16),...]
    unnamed x29 -> x25, local copies, waits for them, and re-layouts: 13.6 us -> 13.7 us
  transfers between devices with their start and end apart: 6 -> 12, of which waited for: 4 -> 8; matrix products, arithmetic and copies ran while one was open for 14% -> 12% of each run, Pallas kernels for 0% -> 0%
where the time goes in v1:
time: 208 us; the launch traced here: 204 us
  waiting for transfers between devices  75.1 us (36%)
  local copies, waits for them, and re-layouts  36.8 us (18%)
  blocking collectives  24.9 us (12%)
  starting transfers between devices  22.8 us (11%)
  matrix products  18.1 us (9%)
  between operations  14.4 us (7%)
  other arithmetic  12.2 us (6%)
    all_to_all x1, waiting for transfers between devices, body(): lax.all_to_all(token_send.reshape(experts, capacity, slice_width), 'dp',...  21.4 us
    all_to_all x1, waiting for transfers between devices, body(): lax.all_to_all(cot_send.reshape(experts, capacity, slice_width), 'dp', sp...  20.4 us
    unnamed x3, waiting for transfers between devices  20.3 us
    psum x1, blocking collectives, body(): combine_grad = lax.psum(comb_part, 'expert')  17 us
    unnamed x25, local copies, waits for them, and re-layouts  13.7 us
    ppermute x7, starting transfers between devices, run_the_values(): oldest = ppermute(oldest, axis_key, [(d, d ^ rr) for d in range(row_out)])  8.19 us
    all_to_all x1, blocking collectives, body(): lax.all_to_all(comb_send.reshape(experts, capacity), 'dp', split_axis=0,...  7.92 us
    dot_general x3, matrix products, contract_first(): lax.dot_general(matrix_a, matrix_b, (((0,), (0,)), ((), ())), preferred_e...  7.47 us
  transfers between devices with their start and end apart: 12, of which 8 were waited for; matrix products, arithmetic and copies ran while one was open for 12% of the time, Pallas kernels for 0%

profile of v1, /device:TPU:0, one launch (start us, length us, event | category | flops | bytes accessed | tf_op | source)
XLA Modules:
  0.0 204.3 jit_solution(14806031349254741105)
XLA Ops:
  12.7 2.8 %gather_fusion = bf16[384,1280]{1,0:T(8,128)(2,1)} fusion(bf16[129,1280]{1,0:T(8,128)(2,1)S(1)} %concatenate.9, s32[1024]{0:T(1024)S(1)} %get-tuple-element.34), kind=kCustom, calls=%fused_computation | custom fusion | bytes 1967616 | tf_op jit(solution)/shard_map/gather | solution.py:68
  15.5 6.3 %all-to-all-start = ((bf16[8,48,1280]{2,1,0:T(8,128)(2,1)}), bf16[8,48,1280]{2,1,0:T(8,128)(2,1)S(1)}, u32[]{:S(2)}, u32[]{:S(2)}) async-start(bf16[8,48,1280]{2,1,0:T(8,128)(2,1)} %bitcast.4), calls=%async_computation | async-start | bytes 1966080 | tf_op jit(solution)/shard_map/all_to_all | solution.py:74
  22.8 2.8 %gather_fusion.1 = bf16[384,1280]{1,0:T(8,128)(2,1)} fusion(bf16[129,1280]{1,0:T(8,128)(2,1)S(1)} %concatenate.10, s32[1024]{0:T(1024)S(1)} %get-tuple-element.34), kind=kCustom, calls=%fused_computation.1 | custom fusion | bytes 1967616 | tf_op jit(solution)/shard_map/gather | solution.py:69
  25.6 21.4 %all-to-all-done = bf16[8,48,1280]{2,1,0:T(8,128)(2,1)S(1)} async-done(((bf16[8,48,1280]{2,1,0:T(8,128)(2,1)}), bf16[8,48,1280]{2,1,0:T(8,128)(2,1)S(1)}, u32[]{:S(2)}, u32[]{:S(2)}) %all-to-all-start) | async-done | bytes 983072 | tf_op jit(solution)/shard_map/all_to_all | solution.py:74
  48.0 3.6 %all-to-all-start.1 = ((bf16[8,48,1280]{2,1,0:T(8,128)(2,1)}), bf16[8,48,1280]{2,1,0:T(8,128)(2,1)S(1)}, u32[]{:S(2)}, u32[]{:S(2)}) async-start(bf16[8,48,1280]{2,1,0:T(8,128)(2,1)} %bitcast.107), calls=%async_computation.1 | async-start | bytes 1966080 | tf_op jit(solution)/shard_map/all_to_all | solution.py:81
  51.6 2.9 %fusion.25 = bf16[384,1,768]{2,0,1:T(8,128)(2,1)S(1)} fusion(bf16[384,1280]{1,0:T(8,128)(2,1)} %bitcast.109, bf16[1,1280,768]{2,1,0:T(8,128)(2,1)} %param.12), kind=kOutput, calls=%fused_computation.29 | convolution fusion | flops 755269632 | bytes 3538944 | tf_op jit(solution)/shard_map/dot_general | solution.py:101
  54.5 1.7 fusion.28
  56.2 20.4 %all-to-all-done.1 = bf16[8,48,1280]{2,1,0:T(8,128)(2,1)S(1)} async-done(((bf16[8,48,1280]{2,1,0:T(8,128)(2,1)}), bf16[8,48,1280]{2,1,0:T(8,128)(2,1)S(1)}, u32[]{:S(2)}, u32[]{:S(2)}) %all-to-all-start.1) | async-done | bytes 983072 | tf_op jit(solution)/shard_map/all_to_all | solution.py:81
  76.6 2.9 %fusion.22 = bf16[384,1,768]{2,0,1:T(8,128)(2,1)S(1)} fusion(bf16[384,1280]{1,0:T(8,128)(2,1)S(1)} %bitcast.106, bf16[1,768,1280]{2,1,0:T(8,128)(2,1)} %param.13), kind=kOutput, calls=%fused_computation.28 | convolution fusion | flops 755269632 | bytes 3538944 | tf_op jit(solution)/shard_map/dot_general | solution.py:29
  80.9 5.2 %copy.32 = bf16[384,3,768]{0,1,2:T(4,128)(2,1)} copy(bf16[384,3,768]{2,0,1:T(8,128)(2,1)} %pad_maximum_fusion) | data formatting | bytes 3538944
  86.2 3.2 %copy.34 = bf16[96,8,3,384]{3,1,2,0:T(8,128)(2,1)} copy(bf16[96,8,3,384]{3,2,1,0:T(4,128)(2,1)} %bitcast.104) | data formatting | bytes 3538944
  89.7 2.8 %gather_fusion.2 = bf16[384]{0:T(512)(128)(2,1)S(1)} fusion(bf16[257]{0:T(512)(128)(2,1)S(1)} %pad_maximum_fusion.2, s32[1024]{0:T(1024)S(1)} %get-tuple-element.33), kind=kCustom, calls=%fused_computation.2 | custom fusion | bytes 3072 | tf_op jit(solution)/shard_map/gather | solution.py:70
  92.6 7.9 %all_to_all.26 = bf16[8,1,48]{2,1,0:T(2,128)(2,1)S(1)} all-to-all(bf16[8,1,48]{2,1,0:T(2,128)(2,1)S(1)} %all_to_all.21), channel_id=1, replica_groups=mesh['expert'=4,'dp'=8] {'dp'}, dimensions={0} | all-to-all | bytes 1536 | tf_op jit(solution)/shard_map/all_to_all | solution.py:88
  100.7 20.2 %reduce-scatter.4.cloned.1.call-done = bf16[192,1152]{1,0:T(8,128)(2,1)} async-done(((bf16[768,1152]{1,0:T(8,128)(2,1)}), bf16[192,1152]{1,0:T(8,128)(2,1)}) %reduce-scatter.4.cloned.1.call-update) | async-done | bytes 442384
  126.0 2.1 %copy.29 = bf16[384,3,192]{0,2,1:T(8,128)(2,1)} copy(bf16[384,3,192]{2,0,1:T(8,128)(2,1)} %pad_maximum_fusion.1) | data formatting | bytes 884736 | tf_op jit(solution)/shard_map/stack | solution.py:114
  129.0 4.6 %all-to-all-start.3 = ((bf16[8,1,48]{2,1,0:T(2,128)(2,1)}), bf16[8,1,48]{2,1,0:T(2,128)(2,1)S(1)}, u32[]{:S(2)}, u32[]{:S(2)}) async-start(bf16[8,1,48]{2,1,0:T(2,128)(2,1)} %convert_element_type.121), calls=%async_computation.3 | async-start | bytes 8192 | tf_op jit(solution)/shard_map/all_to_all | solution.py:128
  135.1 4.0 %all-to-all-done.3 = bf16[8,1,48]{2,1,0:T(2,128)(2,1)S(1)} async-done(((bf16[8,1,48]{2,1,0:T(2,128)(2,1)}), bf16[8,1,48]{2,1,0:T(2,128)(2,1)S(1)}, u32[]{:S(2)}, u32[]{:S(2)}) %all-to-all-start.3) | async-done | bytes 800 | tf_op jit(solution)/shard_map/all_to_all | solution.py:128
  139.2 1.9 gather_fusion.4
  141.3 17.0 %psum.7 = f32[128,2]{1,0:T(8,128)S(1)} all-reduce(f32[128,2]{1,0:T(8,128)S(1)} %reshape.146), channel_id=1, replica_groups=mesh['expert'=4,'dp'=8] {'expert'}, use_global_device_ids=true, to_apply=%region_7.8 | all-reduce | flops 256 | bytes 2048 | tf_op jit(solution)/shard_map/psum | solution.py:141
  159.0 2.7 %all-gather.2.cloned.1.call-done = bf16[384,3,768]{0,2,1:T(8,128)(2,1)} async-done(((bf16[384,3,192]{0,2,1:T(8,128)(2,1)}), bf16[384,3,768]{0,2,1:T(8,128)(2,1)}) %all-gather.2.cloned.1.call-update) | async-done | bytes 1769488 | tf_op jit(solution)/shard_map/all_gather | solution.py:113
  161.6 2.2 %fusion.9 = f32[384,1280]{1,0:T(8,128)S(1)} fusion(bf16[1,1280,768]{2,1,0:T(8,128)(2,1)S(1)} %copy-done, bf16[384,3,768]{0,2,1:T(8,128)(2,1)} %all-gather.2.cloned.1.call-done), kind=kOutput, calls=%fused_computation.19 | convolution fusion | flops 754974720 | bytes 4521984 | tf_op jit(solution)/shard_map/dot_general | solution.py:29
  165.1 1.6 collective-permute-start.1
  167.0 2.3 %collective-permute-start.3 = (bf16[1,48,1280]{2,1,0:T(8,128)(2,1)S(1)}, bf16[1,48,1280]{2,1,0:T(8,128)(2,1)S(1)}, u32[]{:S(2)}, u32[]{:S(2)}) collective-permute-start(bf16[1,48,1280]{2,1,0:T(8,128)(2,1)S(1)} %get-tuple-element.26), channel_id=1, source_target_pairs={{0,4},{1,5},{2,6},{3,7},{4,0},{5,1},{6,2},{7,3},{8,12},{9,13},{10,... | collective-permute-start | bytes 368648 | tf_op jit(solution)/shard_map/ppermute | solution.py:20
  169.6 2.5 %fusion = bf16[1,1280,768]{2,1,0:T(8,128)(2,1)} fusion(bf16[384,1280]{1,0:T(8,128)(2,1)S(1)} %bitcast.111, bf16[384,3,768]{0,2,1:T(8,128)(2,1)S(1)} %copy-done.8), kind=kOutput, calls=%fused_computation.10 | convolution fusion | flops 755957760 | bytes 3538944 | tf_op jit(solution)/shard_map/dot_general | solution.py:35
  172.1 2.5 %fusion.1 = bf16[1,1280,768]{2,1,0:T(8,128)(2,1)} fusion(bf16[384,1280]{1,0:T(8,128)(2,1)S(1)} %bitcast.112, bf16[384,3,768]{0,2,1:T(8,128)(2,1)S(1)} %copy-done.8), kind=kOutput, calls=%fused_computation.11 | convolution fusion | flops 755957760 | bytes 3538944 | tf_op jit(solution)/shard_map/dot_general | solution.py:35
  174.6 2.5 %fusion.2 = bf16[1,768,1280]{2,1,0:T(8,128)(2,1)} fusion(bf16[384,1280]{1,0:T(8,128)(2,1)S(1)} %bitcast.113, bf16[384,3,768]{0,2,1:T(8,128)(2,1)S(1)} %copy-done.8), kind=kOutput, calls=%fused_computation.12 | convolution fusion | flops 755957760 | bytes 3538944 | tf_op jit(solution)/shard_map/dot_general | solution.py:35
  177.1 2.8 %collective-permute-start.5 = (bf16[1,48,1280]{2,1,0:T(8,128)(2,1)S(1)}, bf16[1,48,1280]{2,1,0:T(8,128)(2,1)S(1)}, u32[]{:S(2)}, u32[]{:S(2)}) collective-permute-start(bf16[1,48,1280]{2,1,0:T(8,128)(2,1)S(1)} %get-tuple-element.24), channel_id=1, source_target_pairs={{0,6},{1,7},{2,4},{3,5},{4,2},{5,3},{6,0},{7,1},{8,14},{9,15},{10,... | collective-permute-start | bytes 368648 | tf_op jit(solution)/shard_map/ppermute | solution.py:20
  181.1 3.5 %collective-permute-done.5 = bf16[1,48,1280]{2,1,0:T(8,128)(2,1)S(1)} collective-permute-done((bf16[1,48,1280]{2,1,0:T(8,128)(2,1)S(1)}, bf16[1,48,1280]{2,1,0:T(8,128)(2,1)S(1)}, u32[]{:S(2)}, u32[]{:S(2)}) %collective-permute-start.5) | collective-permute-done | bytes 122912 | tf_op jit(solution)/shard_map/ppermute | solution.py:20
  184.7 2.5 %collective-permute-done.6 = bf16[1,48,1280]{2,1,0:T(8,128)(2,1)S(1)} collective-permute-done((bf16[1,48,1280]{2,1,0:T(8,128)(2,1)S(1)}, bf16[1,48,1280]{2,1,0:T(8,128)(2,1)S(1)}, u32[]{:S(2)}, u32[]{:S(2)}) %collective-permute-start.6) | collective-permute-done | bytes 122912 | tf_op jit(solution)/shard_map/ppermute | solution.py:20
  188.7 3.3 %gather_fusion.3 = f32[256,1280]{1,0:T(8,128)S(1)} fusion(f32[384,1280]{1,0:T(8,128)} %bitcast_convert_fusion, s32[1024]{0:T(1024)S(1)} %pad_clamp_fusion), kind=kCustom, calls=%fused_computation.3 | custom fusion | bytes 2622464 | tf_op jit(solution)/shard_map/gather | solution.py:136
  192.0 1.9 reshape.145
  193.8 3.6 %reduce_sum.31 = bf16[128,1280]{1,0:T(8,128)(2,1)} reduce(f32[128,2,1280]{2,1,0:T(2,128)} %reshape.145, f32[]{:T(128)} %constant.59.clone.1), dimensions={1}, to_apply=%region_5.6 | reduce | flops 163840 | bytes 1638404 | tf_op jit(solution)/shard_map/reduce_sum | solution.py:139
  (82 shorter events, 22.4 us)
Async XLA Ops:
  7.2 47.3 %copy-start = (bf16[1,1280,768]{2,1,0:T(8,128)(2,1)S(1)}, bf16[1,1280,768]{2,1,0:T(8,128)(2,1)}, u32[]{:S(2)}) copy-start(bf16[1,1280,768]{2,1,0:T(8,128)(2,1)} %param.11) | copy-start | bytes 5898244
  15.5 31.5 %all-to-all-start = ((bf16[8,48,1280]{2,1,0:T(8,128)(2,1)}), bf16[8,48,1280]{2,1,0:T(8,128)(2,1)S(1)}, u32[]{:S(2)}, u32[]{:S(2)}) async-start(bf16[8,48,1280]{2,1,0:T(8,128)(2,1)} %bitcast.4), calls=%async_computation | async-start | bytes 1966080 | tf_op jit(solution)/shard_map/all_to_all | solution.py:74
  47.0 0.9 copy-start.2
  48.0 28.7 %all-to-all-start.1 = ((bf16[8,48,1280]{2,1,0:T(8,128)(2,1)}), bf16[8,48,1280]{2,1,0:T(8,128)(2,1)S(1)}, u32[]{:S(2)}, u32[]{:S(2)}) async-start(bf16[8,48,1280]{2,1,0:T(8,128)(2,1)} %bitcast.107), calls=%async_computation.1 | async-start | bytes 1966080 | tf_op jit(solution)/shard_map/all_to_all | solution.py:81
  51.5 69.4 %reduce-scatter.4.cloned.1.call-start = ((), (), s32[]{:S(2)}) async-start(), calls=%async_computation.6 | async-start | bytes 2211840
  51.6 2.9 %copy-start.3 = (bf16[8,48,1280]{2,1,0:T(8,128)(2,1)S(1)}, bf16[8,48,1280]{2,1,0:T(8,128)(2,1)}, u32[]{:S(2)}) copy-start(bf16[8,48,1280]{2,1,0:T(8,128)(2,1)} %copy-done.2) | copy-start | bytes 2949124
  76.6 2.9 %copy-start.1 = (bf16[8,48,1280]{2,1,0:T(8,128)(2,1)}, bf16[8,48,1280]{2,1,0:T(8,128)(2,1)S(1)}, u32[]{:S(2)}) copy-start(bf16[8,48,1280]{2,1,0:T(8,128)(2,1)S(1)} %all-to-all-done.1) | copy-start | bytes 2949124
  76.6 2.9 %copy-start.5 = (bf16[384,1,768]{2,0,1:T(8,128)(2,1)S(1)}, bf16[384,1,768]{2,0,1:T(8,128)(2,1)}, u32[]{:S(2)}) copy-start(bf16[384,1,768]{2,0,1:T(8,128)(2,1)} %fusion.28) | copy-start | bytes 1769476
  86.2 3.3 %copy-start.6 = (bf16[128,2]{0,1:T(2,128)(2,1)S(1)}, bf16[128,2]{0,1:T(2,128)(2,1)}, u32[]{:S(2)}) copy-start(bf16[128,2]{0,1:T(2,128)(2,1)} %param.9) | copy-start | bytes 1540
  89.4 72.3 %all-gather.2.cloned.1.call-start = ((), (), s32[]{:S(2)}) async-start(), calls=%async_computation.5 | async-start | bytes 2211840 | tf_op jit(solution)/shard_map/all_gather | solution.py:113
  129.0 10.1 %all-to-all-start.3 = ((bf16[8,1,48]{2,1,0:T(2,128)(2,1)}), bf16[8,1,48]{2,1,0:T(2,128)(2,1)S(1)}, u32[]{:S(2)}, u32[]{:S(2)}) async-start(bf16[8,1,48]{2,1,0:T(2,128)(2,1)} %convert_element_type.121), calls=%async_computation.3 | async-start | bytes 8192 | tf_op jit(solution)/shard_map/all_to_all | solution.py:128
  161.6 2.2 %copy-start.7 = (bf16[1,1280,768]{2,1,0:T(8,128)(2,1)S(1)}, bf16[1,1280,768]{2,1,0:T(8,128)(2,1)}, u32[]{:S(2)}) copy-start(bf16[1,1280,768]{2,1,0:T(8,128)(2,1)} %param.12) | copy-start | bytes 5898244
  161.6 2.2 %copy-start.8 = (bf16[384,3,768]{0,2,1:T(8,128)(2,1)S(1)}, bf16[384,3,768]{0,2,1:T(8,128)(2,1)}, u32[]{:S(2)}) copy-start(bf16[384,3,768]{0,2,1:T(8,128)(2,1)} %all-gather.2.cloned.1.call-done) | copy-start | bytes 5308420
  164.9 4.7 %copy-start.4 = (bf16[8,48,1280]{2,1,0:T(8,128)(2,1)S(1)}, bf16[8,48,1280]{2,1,0:T(8,128)(2,1)}, u32[]{:S(2)}) copy-start(bf16[8,48,1280]{2,1,0:T(8,128)(2,1)} %copy-done.2) | copy-start | bytes 2949124
  165.0 12.0 %collective-permute-start = (bf16[1,48,1280]{2,1,0:T(8,128)(2,1)S(1)}, bf16[1,48,1280]{2,1,0:T(8,128)(2,1)S(1)}, u32[]{:S(2)}, u32[]{:S(2)}) collective-permute-start(bf16[1,48,1280]{2,1,0:T(8,128)(2,1)S(1)} %get-tuple-element.29), channel_id=1, source_target_pairs={{0,1},{1,0},{2,3},{3,2},{4,5},{5,4},{6,7},{7,6},{8,9},{9,8},{10,11... | collective-permute-start | bytes 368648 | tf_op jit(solution)/shard_map/ppermute | solution.py:20
  165.1 14.8 %collective-permute-start.1 = (bf16[1,48,1280]{2,1,0:T(8,128)(2,1)S(1)}, bf16[1,48,1280]{2,1,0:T(8,128)(2,1)S(1)}, u32[]{:S(2)}, u32[]{:S(2)}) collective-permute-start(bf16[1,48,1280]{2,1,0:T(8,128)(2,1)S(1)} %get-tuple-element.28), channel_id=1, source_target_pairs={{0,2},{1,3},{2,0},{3,1},{4,6},{5,7},{6,4},{7,5},{8,10},{9,11},{10,... | collective-permute-start | bytes 368648 | tf_op jit(solution)/shard_map/ppermute | solution.py:20
  166.7 14.1 %collective-permute-start.2 = (bf16[1,48,1280]{2,1,0:T(8,128)(2,1)S(1)}, bf16[1,48,1280]{2,1,0:T(8,128)(2,1)S(1)}, u32[]{:S(2)}, u32[]{:S(2)}) collective-permute-start(bf16[1,48,1280]{2,1,0:T(8,128)(2,1)S(1)} %get-tuple-element.27), channel_id=1, source_target_pairs={{0,3},{1,2},{2,1},{3,0},{4,7},{5,6},{6,5},{7,4},{8,11},{9,10},{10,... | collective-permute-start | bytes 368648 | tf_op jit(solution)/shard_map/ppermute | solution.py:20
  167.0 13.8 %collective-permute-start.3 = (bf16[1,48,1280]{2,1,0:T(8,128)(2,1)S(1)}, bf16[1,48,1280]{2,1,0:T(8,128)(2,1)S(1)}, u32[]{:S(2)}, u32[]{:S(2)}) collective-permute-start(bf16[1,48,1280]{2,1,0:T(8,128)(2,1)S(1)} %get-tuple-element.26), channel_id=1, source_target_pairs={{0,4},{1,5},{2,6},{3,7},{4,0},{5,1},{6,2},{7,3},{8,12},{9,13},{10,... | collective-permute-start | bytes 368648 | tf_op jit(solution)/shard_map/ppermute | solution.py:20
  169.2 11.9 %collective-permute-start.4 = (bf16[1,48,1280]{2,1,0:T(8,128)(2,1)S(1)}, bf16[1,48,1280]{2,1,0:T(8,128)(2,1)S(1)}, u32[]{:S(2)}, u32[]{:S(2)}) collective-permute-start(bf16[1,48,1280]{2,1,0:T(8,128)(2,1)S(1)} %get-tuple-element.25), channel_id=1, source_target_pairs={{0,5},{1,4},{2,7},{3,6},{4,1},{5,0},{6,3},{7,2},{8,13},{9,12},{10,... | collective-permute-start | bytes 368648 | tf_op jit(solution)/shard_map/ppermute | solution.py:20
  177.1 7.6 %collective-permute-start.5 = (bf16[1,48,1280]{2,1,0:T(8,128)(2,1)S(1)}, bf16[1,48,1280]{2,1,0:T(8,128)(2,1)S(1)}, u32[]{:S(2)}, u32[]{:S(2)}) collective-permute-start(bf16[1,48,1280]{2,1,0:T(8,128)(2,1)S(1)} %get-tuple-element.24), channel_id=1, source_target_pairs={{0,6},{1,7},{2,4},{3,5},{4,2},{5,3},{6,0},{7,1},{8,14},{9,15},{10,... | collective-permute-start | bytes 368648 | tf_op jit(solution)/shard_map/ppermute | solution.py:20
  179.9 7.3 %collective-permute-start.6 = (bf16[1,48,1280]{2,1,0:T(8,128)(2,1)S(1)}, bf16[1,48,1280]{2,1,0:T(8,128)(2,1)S(1)}, u32[]{:S(2)}, u32[]{:S(2)}) collective-permute-start(bf16[1,48,1280]{2,1,0:T(8,128)(2,1)S(1)} %get-tuple-element.23), channel_id=1, source_target_pairs={{0,7},{1,6},{2,5},{3,4},{4,3},{5,2},{6,1},{7,0},{8,15},{9,14},{10,... | collective-permute-start | bytes 368648 | tf_op jit(solution)/shard_map/ppermute | solution.py:20
Sparse Core Ops, SparseCore 0:
  89.5 31.3 reduce-scatter.3
  128.2 33.4 all-gather.1
